TPU v7x, 32 devices: a whole 2x2x4 slice. The times are simulated.
32 devices in a mesh: row: 4 (over x, core), col: 8 (over z, y).
Axes of the slice: x: 2, y: 2, z: 4, core: 2. Of those that a mesh axis runs over, the one named last changes fastest.
Arguments:
- integrals: bfloat16 [384, 64, 4096], P(('row', 'col')), may hold values from -6 to 6
- block_list: int32 [384, 3], P(('row', 'col')), may hold values from 0 to 31, as said below
- p_slot: int32 [16], replicated, may hold values from 0 to 15, as said below
- metric: bfloat16 [16, 64, 64], P('col'), may hold values from -0.75 to 0.75
- density_panel: bfloat16 [2048, 128], P(('row', 'col')), may hold values from -0.75 to 0.75
- pattern: int32 [2048], P(('row', 'col')), may hold values 0 or 1
Outputs:
- exchange_blocks: float32 [2048, 512], P(('row', 'col'))
Inputs may be any that keep to these rules, and one draw needn't show every extreme that they name: `block_list`: rows name (mu block, nu block, auxiliary block). The 12 rows of the device at position row * 8 + col have mu blocks in row * 8 to row * 8 + 7. With owner p_slot[p] // 2, no device lists more than 2 blocks for one owner, and in every row group some owner gets exactly 2 from every device of the group. A permutation; auxiliary block p is contracted by col index p_slot[p] // 2, local slot p_slot[p] % 2.
All inputs are finite; a program needn't handle non-finite values. No bound on the sum of `pattern` on one device may be relied on, other than what follows from the above.
Results may differ from a plain program's by a relative error of at most 0.00059.
Values may be sent and summed in bfloat16 or wider, within the bound.
A program may use at most 192 MiB of HBM per device.

v0:
```python
import jax
import jax.numpy as jnp
from jax import lax
from jax.sharding import PartitionSpec as P

MB = 8
CAP = 2


def on_device(integrals, block_list, p_slot, metric, density_panel, pattern):
    columns = lax.axis_size("col")
    owned_slots = metric.shape[0]
    block_size = metric.shape[1]
    listed = integrals.shape[0]
    panel_width = density_panel.shape[1]
    total_slots = columns * CAP
    all_slots = owned_slots * columns
    row_here = lax.axis_index("row")
    first_ids = block_list[:, 0] - row_here * MB
    second_ids = block_list[:, 1]
    fitting_ids = block_list[:, 2]
    slot_match = fitting_ids[:, None] == jnp.arange(all_slots, dtype=jnp.int32)[None, :]
    slot_ids = jnp.sum(jnp.where(slot_match, p_slot[None, :], 0), axis=1)
    owners = slot_ids // owned_slots
    local_slot = slot_ids % owned_slots
    same_owner = owners[:, None] == owners[None, :]
    before = jnp.arange(listed)[None, :] < jnp.arange(listed)[:, None]
    position = jnp.sum(same_owner & before, axis=1)
    target = owners * CAP + position
    slot_hits = jnp.arange(total_slots, dtype=jnp.int32)[:, None] == target[None, :]
    placing = slot_hits.astype(jnp.bfloat16)
    outgoing = jnp.dot(
        placing, integrals.reshape(listed, -1), preferred_element_type=jnp.float32
    ).astype(jnp.bfloat16)
    outgoing = outgoing.reshape(columns, CAP, block_size, block_size * block_size)
    labels = jnp.stack([first_ids, local_slot, second_ids, jnp.ones_like(first_ids)], axis=1)
    label_send = jnp.sum(jnp.where(slot_hits[:, :, None], labels[None, :, :], 0), axis=1).astype(
        jnp.bfloat16
    )
    label_send = label_send.reshape(columns, CAP, 4)
    arrived, arrived_labels = (
        lax.all_to_all(outgoing, "col", split_axis=0, concat_axis=0, tiled=True),
        lax.all_to_all(label_send, "col", split_axis=0, concat_axis=0, tiled=True),
    )
    arrived = arrived.reshape(total_slots, block_size, block_size * block_size)
    arrived_labels = arrived_labels.astype(jnp.int32).reshape(total_slots, 4)
    first_in = arrived_labels[:, 0]
    slot_in = arrived_labels[:, 1]
    second_in = arrived_labels[:, 2]
    flag_in = arrived_labels[:, 3]
    picking = (
        (slot_in[:, None] == jnp.arange(owned_slots, dtype=jnp.int32)[None, :])
        & (flag_in[:, None] > 0)
    ).astype(jnp.bfloat16)
    chosen = jnp.einsum("es,sqp->eqp", picking, metric, preferred_element_type=jnp.float32).astype(
        jnp.bfloat16
    )
    applied = jnp.einsum(
        "eqp,eqx->epx", chosen, arrived, preferred_element_type=jnp.float32
    ).astype(jnp.bfloat16)
    kept = jnp.where(pattern[:, None] > 0, density_panel, jnp.zeros_like(density_panel))
    panel_all = lax.all_gather(kept, ("row", "col"), axis=0, tiled=True)
    panel_all = panel_all.reshape(-1, block_size, panel_width)
    group_size = 4
    group_count = total_slots // group_size
    pair_count = owned_slots * MB
    pair_keys = slot_in * MB + first_in
    anchor = jnp.zeros((), jnp.int32)

    def accumulate(running, inputs_now):
        blocks, second, keyed = inputs_now
        for member in range(group_size):
            flat = blocks[member].reshape(block_size * block_size, block_size)
            contrib = jnp.dot(flat, panel_all[second[member]], preferred_element_type=jnp.float32)
            corner = (keyed[member], anchor, anchor, anchor)
            current = lax.dynamic_slice(running, corner, (1, block_size, block_size, panel_width))
            updated = current + contrib.reshape(1, block_size, block_size, panel_width)
            running = lax.dynamic_update_slice(running, updated, corner)
        return (running, None)

    empty_sum = jnp.zeros((pair_count, block_size, block_size, panel_width), jnp.float32)
    grouped = (
        applied.reshape(group_count, group_size, block_size, block_size * block_size),
        second_in.reshape(group_count, group_size),
        pair_keys.reshape(group_count, group_size),
    )
    filled, _ = lax.scan(accumulate, empty_sum, grouped)
    rounded = filled.astype(jnp.bfloat16).reshape(
        owned_slots, MB, block_size, block_size, panel_width
    )
    local_tile = jnp.einsum(
        "jupmo,jvpno->umvn", rounded, rounded, preferred_element_type=jnp.float32
    )
    local_tile = local_tile.reshape(MB * block_size, MB * block_size) * (
        1.0 / (all_slots * block_size * panel_width)
    )
    summed = lax.psum(local_tile, "col")
    share_rows = summed.shape[0] // columns
    result_rows = lax.dynamic_slice_in_dim(
        summed, lax.axis_index("col") * share_rows, share_rows, 0
    )
    return result_rows


def solution(mesh):
    placed = (
        P(("row", "col"), None, None),
        P(("row", "col"), None),
        P(),
        P("col", None, None),
        P(("row", "col"), None),
        P(("row", "col")),
    )
    return jax.shard_map(
        on_device, mesh=mesh, in_specs=placed, out_specs=P(("row", "col"), None), check_vma=False
    )
```

profile of v0, /device:TPU:0, one launch (start us, length us, event | category | flops | bytes accessed | tf_op | source)
XLA Modules:
  0.0 590.8 jit_solution(5425671029016775812)
XLA Ops:
  6.5 0.8 slice_subtract_fusion
  7.3 0.8 select_reduce_fusion.1
  8.7 0.7 copy.12
  9.4 7.3 %all-to-all-start = ((bf16[8,2,4]{2,1,0:T(2,128)(2,1)}), bf16[8,2,4]{2,1,0:T(2,128)(2,1)S(1)}, u32[]{:S(2)}, u32[]{:S(2)}) async-start(bf16[8,2,4]{2,1,0:T(2,128)(2,1)} %bitcast.22), calls=%async_computation | async-start | bytes 8192 | tf_op jit(solution)/shard_map/all_to_all | solution.py:43
  16.7 7.2 %pad.4 = bf16[16,64,4096]{2,1,0:T(8,128)(2,1)} pad(bf16[12,64,4096]{2,1,0:T(8,128)(2,1)} %param.8, bf16[]{:T(256)} %constant.62.clone.1), padding=0_4x0_0x0_0 | pad | bytes 14680066
  23.8 11.2 %copy.17 = bf16[2,8,64,4096]{3,1,2,0:T(8,128)(2,1)} copy(bf16[2,8,64,4096]{3,2,1,0:T(8,128)(2,1)} %bitcast.130) | data formatting | bytes 16777216
  35.0 6.9 %convolution_convert_fusion = bf16[16,262144]{1,0:T(8,128)(2,1)} fusion(bf16[12,262144]{1,0:T(8,128)(2,1)} %bitcast.127, s32[12]{0:T(128)S(1)} %multiply_add_fusion), kind=kOutput, calls=%fused_computation.26 | convolution fusion | flops 104857792 | bytes 14680112 | tf_op jit(solution)/shard_map/dot_general | solution.py:32
  41.9 11.2 %copy.18 = bf16[2,8,64,4096]{3,2,1,0:T(8,128)(2,1)} copy(bf16[2,8,64,4096]{3,1,2,0:T(8,128)(2,1)} %bitcast.128) | data formatting | bytes 16777216
  53.1 6.1 %all-to-all-start.1 = ((bf16[8,2,64,4096]{3,2,1,0:T(8,128)(2,1)}), bf16[8,2,64,4096]{3,2,1,0:T(8,128)(2,1)}, u32[]{:S(2)}, u32[]{:S(2)}) async-start(bf16[8,2,64,4096]{3,2,1,0:T(8,128)(2,1)} %bitcast.129), calls=%async_computation.1 | async-start | bytes 16777216 | tf_op jit(solution)/shard_map/all_to_all | solution.py:42
  59.4 245.5 %all_gather.3 = bf16[2048,128]{1,0:T(8,128)(2,1)} all-gather(bf16[64,128]{1,0:T(8,128)(2,1)S(1)} %broadcast_select_fusion), channel_id=1, replica_groups=mesh['row'=4,'col'=8] {'row','col'}, dimensions={0}, use_global_device_ids=true | all-gather | bytes 540672 | tf_op jit(solution)/shard_map/all_gather | solution.py:62
  304.9 0.2 slice_reduce_fusion
  305.5 0.3 convolution_convert_fusion.2
  305.8 9.0 %convolution_convert_fusion.1 = bf16[16,64,4096]{2,1,0:T(8,128)(2,1)} fusion(bf16[16,64,4096]{2,1,0:T(8,128)(2,1)} %bitcast.26, bf16[16,64,64]{2,0,1:T(8,128)(2,1)S(1)} %convolution_convert_fusion.2), kind=kOutput, calls=%fused_computation.27 | convolution fusion | flops 541065216 | bytes 16908288 | tf_op jit(solution)/shard_map/eqp,eqx->epx/dot_general | solution.py:58
  314.8 11.2 %broadcast_in_dim.58 = f32[16,64,64,128]{3,2,1,0:T(8,128)} broadcast(f32[]{:T(128)} %constant.56.clone.1), dimensions={} | broadcast | bytes 33554436 | tf_op jit(solution)/shard_map/broadcast_in_dim | solution.py:81
  326.0 143.0 %while.10 = (s32[]{:T(128)}, f32[16,64,64,128]{3,2,1,0:T(8,128)}, s32[4,4]{1,0:T(4,128)S(1)}, bf16[4,4,64,4096]{3,2,1,0:T(8,128)(2,1)}, s32[4,4]{1,0:T(4,128)S(1...) while((s32[]{:T(128)}, f32[16,64,64,128]{3,2,1,0:T(8,128)}, ...), condition=%wide.region_4.5_spmd, body=%wide.region_3.4_spmd.sunk | while | flops 270532608 | bytes 27329120 | solution.py:87
  326.0 0.7 fusion.62
  328.6 0.7 fusion.61
  330.9 1.7 constant_dynamic-slice_fusion.10
  332.6 1.1 reshape.216
  333.7 3.4 fusion.63
  340.5 1.1 reshape.217
  341.6 3.4 fusion.64
  349.0 1.1 reshape.218
  350.2 3.4 fusion.65
  357.4 1.1 reshape.219
  358.5 3.3 fusion.66
  361.8 0.7 fusion.62
  364.4 0.7 fusion.61
  366.7 1.7 constant_dynamic-slice_fusion.10
  368.4 1.1 reshape.216
  369.5 3.4 fusion.63
  376.2 1.1 reshape.217
  377.4 3.4 fusion.64
  384.8 1.1 reshape.218
  385.9 3.4 fusion.65
  393.1 1.1 reshape.219
  394.2 3.4 fusion.66
  397.6 0.7 fusion.62
  400.1 0.7 fusion.61
  402.5 1.7 constant_dynamic-slice_fusion.10
  404.1 1.1 reshape.216
  405.3 3.4 fusion.63
  412.0 1.1 reshape.217
  413.1 3.4 fusion.64
  420.6 1.1 reshape.218
  421.7 3.4 fusion.65
  428.8 1.1 reshape.219
  429.9 3.3 fusion.66
  433.3 0.7 fusion.62
  435.8 0.7 fusion.61
  438.1 1.7 constant_dynamic-slice_fusion.10
  439.8 1.1 reshape.216
  440.9 3.4 fusion.63
  447.7 1.1 reshape.217
  448.8 3.4 fusion.64
  456.2 1.1 reshape.218
  457.4 3.4 fusion.65
  464.5 1.1 reshape.219
  465.6 3.4 fusion.66
  469.0 12.8 %convert_element_type.31 = bf16[16,64,64,128]{3,2,1,0:T(8,128)(2,1)S(1)} convert(f32[16,64,64,128]{3,2,1,0:T(8,128)} %get-tuple-element.37) | non-fusion elementwise | flops 8388608 | bytes 50331648 | tf_op jit(solution)/shard_map/convert_element_type | solution.py:88
  481.8 7.0 %copy.15 = bf16[8,64,2,128,64]{3,1,0,4,2:T(8,128)(2,1)} copy(bf16[8,64,2,128,64]{3,1,4,0,2:T(8,128)(2,1)S(1)} %bitcast.126) | data formatting | bytes 33554432 | tf_op jit(solution)/shard_map/jupmo,jvpno->umvn/dot_general | solution.py:91
  488.9 18.0 %fusion.16 = f32[512,512]{1,0:T(8,128)} fusion(bf16[512,2,128,64]{2,0,3,1:T(8,128)(2,1)} %bitcast.131), kind=kOutput, calls=%fused_computation.29 | convolution fusion | flops 8590196736 | bytes 17825792 | tf_op jit(solution)/shard_map/jupmo,jvpno->umvn/dot_general | solution.py:91
  506.9 75.4 %all-reduce.2.cloned.1.call-done = f32[512,512]{1,0:T(8,128)} async-done(((f32[512,512]{1,0:T(8,128)}), f32[512,512]{1,0:T(8,128)}) %all-reduce.2.cloned.1.call-update) | async-done | bytes 1048592 | tf_op jit(solution)/shard_map/psum | solution.py:97
  582.4 1.6 constant_dynamic-slice_fusion.6
  (32 shorter events, 1.0 us)
Async XLA Ops:
  6.5 299.0 %copy-start = (bf16[2,64,64]{2,1,0:T(8,128)(2,1)S(1)}, bf16[2,64,64]{2,1,0:T(8,128)(2,1)}, u32[]{:S(2)}) copy-start(bf16[2,64,64]{2,1,0:T(8,128)(2,1)} %param.11) | copy-start | bytes 49156
  9.4 43.7 %all-to-all-start = ((bf16[8,2,4]{2,1,0:T(2,128)(2,1)}), bf16[8,2,4]{2,1,0:T(2,128)(2,1)S(1)}, u32[]{:S(2)}, u32[]{:S(2)}) async-start(bf16[8,2,4]{2,1,0:T(2,128)(2,1)} %bitcast.22), calls=%async_computation | async-start | bytes 8192 | tf_op jit(solution)/shard_map/all_to_all | solution.py:43
  53.1 6.2 %copy-start.3 = (s32[64]{0:T(128)S(1)}, s32[64]{0:T(128)}, u32[]{:S(2)}) copy-start(s32[64]{0:T(128)} %param.13) | copy-start | bytes 772
  53.1 6.2 %copy-start.2 = (bf16[64,128]{1,0:T(8,128)(2,1)S(1)}, bf16[64,128]{1,0:T(8,128)(2,1)}, u32[]{:S(2)}) copy-start(bf16[64,128]{1,0:T(8,128)(2,1)} %param.12) | copy-start | bytes 49156
  53.1 252.7 %all-to-all-start.1 = ((bf16[8,2,64,4096]{3,2,1,0:T(8,128)(2,1)}), bf16[8,2,64,4096]{3,2,1,0:T(8,128)(2,1)}, u32[]{:S(2)}, u32[]{:S(2)}) async-start(bf16[8,2,64,4096]{3,2,1,0:T(8,128)(2,1)} %bitcast.129), calls=%async_computation.1 | async-start | bytes 16777216 | tf_op jit(solution)/shard_map/all_to_all | solution.py:42
  59.3 523.1 %all-reduce.2.cloned.1.call-start = ((), (), s32[]{:S(2)}) async-start(), calls=%async_computation.2 | async-start | bytes 2097152 | tf_op jit(solution)/shard_map/psum | solution.py:97
  488.9 95.1 %copy-start.1 = (bf16[2,64,64]{2,1,0:T(8,128)(2,1)S(1)}, bf16[2,64,64]{2,1,0:T(8,128)(2,1)}, u32[]{:S(2)}) copy-start(bf16[2,64,64]{2,1,0:T(8,128)(2,1)} %param.11) | copy-start | bytes 49156
Sparse Core Ops, SparseCore 0:
  507.1 75.2 all-reduce.1
where the time goes:
time: 593 us; the launch traced here: 591 us
  blocking collectives  246 us (41%)
  matrix products  88.2 us (15%)
  local copies, waits for them, and re-layouts  80.2 us (14%)
  waiting for transfers between devices  75.4 us (13%)
  loops' own time  59.1 us (10%)
  other arithmetic  15.3 us (3%)
  starting transfers between devices  13.5 us (2%)
  between operations  13.5 us (2%)
    all_gather x1, blocking collectives, on_device(): panel_all = lax.all_gather(kept, ('row', 'col'), axis=0, tiled=True)  246 us
    psum x1, waiting for transfers between devices, on_device(): summed = lax.psum(local_tile, 'col')  75.4 us
    another operation x1, loops' own time, on_device(): filled, _ = lax.scan(accumulate, empty_sum, grouped)  59.1 us
    dot_general x16, matrix products, accumulate(): jnp.dot(flat, panel_all[second[member]], preferred_element_type=jnp.float32)  54 us
    unnamed x11, local copies, waits for them, and re-layouts  29.5 us
    dot_general x1, matrix products, on_device(): jnp.einsum('jupmo,jvpno->umvn', rounded, rounded, preferred_element_type=...  18 us
    another operation x16, local copies, waits for them, and re-layouts  18 us
    convert_element_type x1, other arithmetic, on_device(): filled.astype(jnp.bfloat16)  12.8 us
  transfers between devices with their start and end apart: 3, of which 1 were waited for; matrix products, arithmetic and copies ran while one was open for 6% of the time, Pallas kernels for 0%

commit v1 on v0

--- a/solution.py
+++ b/solution.py
@@ -94,7 +94,8 @@
     local_tile = local_tile.reshape(MB * block_size, MB * block_size) * (
         1.0 / (all_slots * block_size * panel_width)
     )
-    summed = lax.psum(local_tile, "col")
+    parts = lax.all_gather(local_tile, "col", axis=0, tiled=False)
+    summed = parts.sum(axis=0)
     share_rows = summed.shape[0] // columns
     result_rows = lax.dynamic_slice_in_dim(
         summed, lax.axis_index("col") * share_rows, share_rows, 0

time: 593 us -> 643 us (1.084)
  waiting for transfers between devices: 75.4 us -> 122 us
    all_gather x0 -> x1, waiting for transfers between devices: none -> 122 us  [on_device(): parts = lax.all_gather(local_tile, 'col', axis=0, tiled=False)]
    psum x1 -> x0, waiting for transfers between devices: 75.4 us -> none  [on_device(): summed = lax.psum(local_tile, 'col')]
where the time goes in v1:
time: 643 us; the launch traced here: 641 us
  blocking collectives  246 us (38%)
  waiting for transfers between devices  122 us (19%)
  matrix products  88.2 us (14%)
  local copies, waits for them, and re-layouts  79.3 us (12%)
  loops' own time  59.1 us (9%)
  other arithmetic  19.8 us (3%)
  starting transfers between devices  13.5 us (2%)
  between operations  13.5 us (2%)
    all_gather x1, blocking collectives, on_device(): panel_all = lax.all_gather(kept, ('row', 'col'), axis=0, tiled=True)  246 us
    all_gather x1, waiting for transfers between devices, on_device(): parts = lax.all_gather(local_tile, 'col', axis=0, tiled=False)  122 us
    another operation x1, loops' own time, on_device(): filled, _ = lax.scan(accumulate, empty_sum, grouped)  59.1 us
    dot_general x16, matrix products, accumulate(): jnp.dot(flat, panel_all[second[member]], preferred_element_type=jnp.float32)  54 us
    unnamed x11, local copies, waits for them, and re-layouts  29.5 us
    dot_general x1, matrix products, on_device(): jnp.einsum('jupmo,jvpno->umvn', rounded, rounded, preferred_element_type=...  18 us
    another operation x16, local copies, waits for them, and re-layouts  18 us
  transfers between devices with their start and end apart: 3, of which 1 were waited for; matrix products, arithmetic and copies ran while one was open for 6% of the time, Pallas kernels for 0%

profile of v1, /device:TPU:0, one launch (start us, length us, event | category | flops | bytes accessed | tf_op | source)
XLA Modules:
  0.0 640.5 jit_solution(17182884477582610609)
XLA Ops:
  6.5 0.8 slice_subtract_fusion
  7.3 0.8 select_reduce_fusion.1
  8.7 0.7 copy.12
  9.4 7.3 %all-to-all-start = ((bf16[8,2,4]{2,1,0:T(2,128)(2,1)}), bf16[8,2,4]{2,1,0:T(2,128)(2,1)S(1)}, u32[]{:S(2)}, u32[]{:S(2)}) async-start(bf16[8,2,4]{2,1,0:T(2,128)(2,1)} %bitcast.22), calls=%async_computation | async-start | bytes 8192 | tf_op jit(solution)/shard_map/all_to_all | solution.py:43
  16.7 7.2 %pad.4 = bf16[16,64,4096]{2,1,0:T(8,128)(2,1)} pad(bf16[12,64,4096]{2,1,0:T(8,128)(2,1)} %param.8, bf16[]{:T(256)} %constant.63.clone.1), padding=0_4x0_0x0_0 | pad | bytes 14680066
  23.8 11.2 %copy.17 = bf16[2,8,64,4096]{3,1,2,0:T(8,128)(2,1)} copy(bf16[2,8,64,4096]{3,2,1,0:T(8,128)(2,1)} %bitcast.131) | data formatting | bytes 16777216
  35.0 6.9 %convolution_convert_fusion = bf16[16,262144]{1,0:T(8,128)(2,1)} fusion(bf16[12,262144]{1,0:T(8,128)(2,1)} %bitcast.128, s32[12]{0:T(128)S(1)} %multiply_add_fusion), kind=kOutput, calls=%fused_computation.26 | convolution fusion | flops 104857792 | bytes 14680112 | tf_op jit(solution)/shard_map/dot_general | solution.py:32
  41.9 11.2 %copy.18 = bf16[2,8,64,4096]{3,2,1,0:T(8,128)(2,1)} copy(bf16[2,8,64,4096]{3,1,2,0:T(8,128)(2,1)} %bitcast.129) | data formatting | bytes 16777216
  53.1 6.1 all-to-all-start.1
  59.4 245.5 %all_gather.9 = bf16[2048,128]{1,0:T(8,128)(2,1)} all-gather(bf16[64,128]{1,0:T(8,128)(2,1)S(1)} %broadcast_select_fusion), channel_id=1, replica_groups=mesh['row'=4,'col'=8] {'row','col'}, dimensions={0}, use_global_device_ids=true | all-gather | bytes 540672 | tf_op jit(solution)/shard_map/all_gather | solution.py:62
  305.5 0.3 convolution_convert_fusion.2
  305.8 9.0 %convolution_convert_fusion.1 = bf16[16,64,4096]{2,1,0:T(8,128)(2,1)} fusion(bf16[16,64,4096]{2,1,0:T(8,128)(2,1)} %bitcast.26, bf16[16,64,64]{2,0,1:T(8,128)(2,1)S(1)} %convolution_convert_fusion.2), kind=kOutput, calls=%fused_computation.27 | convolution fusion | flops 541065216 | bytes 16908288 | tf_op jit(solution)/shard_map/eqp,eqx->epx/dot_general | solution.py:58
  314.8 11.2 %broadcast_in_dim.58 = f32[16,64,64,128]{3,2,1,0:T(8,128)} broadcast(f32[]{:T(128)} %constant.39.clone.1), dimensions={} | broadcast | bytes 33554436 | tf_op jit(solution)/shard_map/broadcast_in_dim | solution.py:81
  326.0 143.0 %while.10 = (s32[]{:T(128)}, f32[16,64,64,128]{3,2,1,0:T(8,128)}, s32[4,4]{1,0:T(4,128)S(1)}, bf16[4,4,64,4096]{3,2,1,0:T(8,128)(2,1)}, s32[4,4]{1,0:T(4,128)S(1...) while((s32[]{:T(128)}, f32[16,64,64,128]{3,2,1,0:T(8,128)}, ...), condition=%wide.region_4.5_spmd, body=%wide.region_3.4_spmd.sunk | while | flops 270532608 | bytes 27329120 | solution.py:87
  326.0 0.7 fusion.62
  328.6 0.7 fusion.61
  330.9 1.7 constant_dynamic-slice_fusion.10
  332.6 1.1 reshape.217
  333.7 3.4 fusion.63
  340.5 1.1 reshape.218
  341.6 3.4 fusion.64
  349.0 1.1 reshape.219
  350.2 3.4 fusion.65
  357.4 1.1 reshape.220
  358.5 3.3 fusion.66
  361.8 0.7 fusion.62
  364.4 0.7 fusion.61
  366.7 1.7 constant_dynamic-slice_fusion.10
  368.4 1.1 reshape.217
  369.5 3.4 fusion.63
  376.2 1.1 reshape.218
  377.4 3.4 fusion.64
  384.8 1.1 reshape.219
  385.9 3.4 fusion.65
  393.1 1.1 reshape.220
  394.2 3.4 fusion.66
  397.6 0.7 fusion.62
  400.1 0.7 fusion.61
  402.5 1.7 constant_dynamic-slice_fusion.10
  404.1 1.1 reshape.217
  405.3 3.4 fusion.63
  412.0 1.1 reshape.218
  413.1 3.4 fusion.64
  420.6 1.1 reshape.219
  421.7 3.4 fusion.65
  428.8 1.1 reshape.220
  429.9 3.3 fusion.66
  433.3 0.7 fusion.62
  435.8 0.7 fusion.61
  438.1 1.7 constant_dynamic-slice_fusion.10
  439.8 1.1 reshape.217
  440.9 3.4 fusion.63
  447.7 1.1 reshape.218
  448.8 3.4 fusion.64
  456.2 1.1 reshape.219
  457.4 3.4 fusion.65
  464.5 1.1 reshape.220
  465.6 3.4 fusion.66
  469.0 12.8 %convert_element_type.31 = bf16[16,64,64,128]{3,2,1,0:T(8,128)(2,1)S(1)} convert(f32[16,64,64,128]{3,2,1,0:T(8,128)} %get-tuple-element.37) | non-fusion elementwise | flops 8388608 | bytes 50331648 | tf_op jit(solution)/shard_map/convert_element_type | solution.py:88
  481.8 7.0 %copy.15 = bf16[8,64,2,128,64]{3,1,0,4,2:T(8,128)(2,1)} copy(bf16[8,64,2,128,64]{3,1,4,0,2:T(8,128)(2,1)S(1)} %bitcast.127) | data formatting | bytes 33554432 | tf_op jit(solution)/shard_map/jupmo,jvpno->umvn/dot_general | solution.py:91
  488.9 18.0 %fusion.16 = f32[512,512]{1,0:T(8,128)} fusion(bf16[512,2,128,64]{2,0,3,1:T(8,128)(2,1)} %bitcast.132), kind=kOutput, calls=%fused_computation.29 | convolution fusion | flops 8590196736 | bytes 17825792 | tf_op jit(solution)/shard_map/jupmo,jvpno->umvn/dot_general | solution.py:91
  506.9 121.6 %all-gather.3.cloned.1.call-done = f32[4096,512]{1,0:T(8,128)} async-done(((f32[512,512]{1,0:T(8,128)}), f32[4096,512]{1,0:T(8,128)}) %all-gather.3.cloned.1.call-update) | async-done | bytes 8388624 | tf_op jit(solution)/shard_map/all_gather | solution.py:97
  628.5 4.5 reduce_sum.42
  633.0 0.7 constant_dynamic-slice_fusion.6
  (33 shorter events, 1.2 us)
Async XLA Ops:
  6.5 299.0 %copy-start = (bf16[2,64,64]{2,1,0:T(8,128)(2,1)S(1)}, bf16[2,64,64]{2,1,0:T(8,128)(2,1)}, u32[]{:S(2)}) copy-start(bf16[2,64,64]{2,1,0:T(8,128)(2,1)} %param.11) | copy-start | bytes 49156
  9.4 43.7 %all-to-all-start = ((bf16[8,2,4]{2,1,0:T(2,128)(2,1)}), bf16[8,2,4]{2,1,0:T(2,128)(2,1)S(1)}, u32[]{:S(2)}, u32[]{:S(2)}) async-start(bf16[8,2,4]{2,1,0:T(2,128)(2,1)} %bitcast.22), calls=%async_computation | async-start | bytes 8192 | tf_op jit(solution)/shard_map/all_to_all | solution.py:43
  53.1 6.2 copy-start.3
  53.1 6.2 copy-start.2
  53.1 252.7 %all-to-all-start.1 = ((bf16[8,2,64,4096]{3,2,1,0:T(8,128)(2,1)}), bf16[8,2,64,4096]{3,2,1,0:T(8,128)(2,1)}, u32[]{:S(2)}, u32[]{:S(2)}) async-start(bf16[8,2,64,4096]{3,2,1,0:T(8,128)(2,1)} %bitcast.130), calls=%async_computation.1 | async-start | bytes 16777216 | tf_op jit(solution)/shard_map/all_to_all | solution.py:42
  59.3 569.2 %all-gather.3.cloned.1.call-start = ((), (), s32[]{:S(2)}) async-start(), calls=%async_computation.2 | async-start | bytes 9437184 | tf_op jit(solution)/shard_map/all_gather | solution.py:97
  488.9 144.8 %copy-start.1 = (bf16[2,64,64]{2,1,0:T(8,128)(2,1)S(1)}, bf16[2,64,64]{2,1,0:T(8,128)(2,1)}, u32[]{:S(2)}) copy-start(bf16[2,64,64]{2,1,0:T(8,128)(2,1)} %param.11) | copy-start | bytes 49156
Sparse Core Ops, SparseCore 0:
  507.1 121.4 all-gather.2
